TPU v7x, 32 devices: a whole 2x2x4 slice. The times are simulated.
32 devices in a mesh: light: 4 (over z), pix: 4 (over x, core), cam: 2 (over y).
Axes of the slice: x: 2, y: 2, z: 4, core: 2. Of those that a mesh axis runs over, the one named last changes fastest.
Arguments:
- reflectance: bfloat16 [1024, 32, 4096], P('light', 'cam', 'pix'), may hold values from -120 to 120
- start_basis: float32 [1024, 128], replicated, may hold values from -6 to 6
Outputs:
- core_tensor: float32 [128, 32, 4096], P('light', 'cam', 'pix')
- light_basis: float32 [1024, 128], P('light')
All inputs are finite; a program needn't handle non-finite values.
Results may differ from a plain program's by a relative error of at most 0.015.
Values may be sent and summed in bfloat16 or wider, within the bound.
A program may use at most 128 MiB of HBM per device.

v0:
```python
import jax
import jax.numpy as jnp
from jax import lax
from jax.sharding import PartitionSpec as P

ITERS = 2


def orthonormal(image_full):
    inner_gram = jnp.dot(
        image_full.T,
        image_full,
        preferred_element_type=jnp.float32,
        precision=lax.Precision.HIGHEST,
    )
    factor = jnp.linalg.cholesky(inner_gram)
    return lax.linalg.triangular_solve(
        factor, image_full, left_side=False, lower=True, transpose_a=True
    )


def per_device(reflectance, start_basis):
    light_rows, camera_cols, pixels = reflectance.shape
    rank_total = start_basis.shape[1]
    light_count = lax.axis_size("light")
    position = lax.axis_index("light")
    inverse_cols = 1.0 / (camera_cols * pixels * lax.axis_size("cam") * lax.axis_size("pix"))
    fibers = reflectance.reshape(light_rows, camera_cols * pixels)
    full_gram = None
    exchanged = None
    exchanged = lax.all_to_all(reflectance, "light", split_axis=2, concat_axis=0, tiled=True)
    gathered = exchanged.reshape(light_rows * light_count, -1)
    own_gram = lax.dot_general(
        gathered, gathered, (((1,), (1,)), ((), ())), preferred_element_type=jnp.float32
    )
    full_gram = lax.psum(own_gram, ("light", "pix", "cam")) * inverse_cols
    gram_rows = lax.dynamic_slice_in_dim(full_gram, position * light_rows, light_rows, 0)
    basis_now = start_basis
    for iteration in range(ITERS):
        image_rows = jnp.dot(
            gram_rows,
            basis_now,
            preferred_element_type=jnp.float32,
            precision=lax.Precision.HIGHEST,
        )
        image_full = lax.all_gather(
            image_rows.astype(jnp.bfloat16), "light", axis=0, tiled=True
        ).astype(image_rows.dtype)
        basis_now = orthonormal(image_full)
    basis_rows = lax.dynamic_slice_in_dim(basis_now, position * light_rows, light_rows, 0)
    rank_rows = rank_total // light_count
    rounded = basis_rows.astype(jnp.bfloat16)
    core_rows = lax.psum_scatter(
        lax.dot_general(
            rounded, fibers, (((0,), (0,)), ((), ())), preferred_element_type=jnp.float32
        ).astype(jnp.bfloat16),
        "light",
        scatter_dimension=0,
        tiled=True,
    ).astype(jnp.float32)
    return (core_rows.reshape(rank_rows, camera_cols, pixels), basis_rows)


def solution(mesh):
    placed = (P("light", "cam", "pix"), P())
    return jax.shard_map(
        per_device,
        mesh=mesh,
        in_specs=placed,
        out_specs=(P("light", "cam", "pix"), P("light", None)),
        check_vma=False,
    )
```

profile of v0, /device:TPU:0, one launch (start us, length us, event | category | flops | bytes accessed | tf_op | source)
XLA Modules:
  0.0 573.3 jit_solution(15910480420709180516)
XLA Ops:
  7.2 0.0 copy-start
  7.2 0.0 all-reduce.2.cloned.1.call-start
  7.2 13.4 %copy.16 = bf16[256,16,1024]{0,1,2:T(8,128)(2,1)} copy(bf16[256,16,1024]{2,1,0:T(8,128)(2,1)} %param.5) | data formatting | bytes 16777216 | tf_op args[0]
  20.7 192.2 %all_to_all.15 = bf16[256,16,1024]{0,1,2:T(8,128)(2,1)} all-to-all(bf16[256,16,1024]{0,1,2:T(8,128)(2,1)} %copy.16), channel_id=1, replica_groups=mesh['light'=4,'pix'=4,'cam'=2] {'light'}, dimensions={2} | all-to-all | bytes 16777216 | tf_op jit(solution)/shard_map/all_to_all | solution.py:31
  212.9 16.0 %copy.17 = bf16[256,16,4,256]{3,1,0,2:T(8,128)(2,1)} copy(bf16[256,16,4,256]{0,1,3,2:T(8,128)(2,1)} %bitcast.43) | data formatting | bytes 16777216 | tf_op jit(solution)/shard_map/all_to_all | solution.py:31
  228.9 12.2 %copy.21 = bf16[128,8,16,256]{3,1,2,0:T(8,128)(2,1)} copy(bf16[128,8,16,256]{3,2,1,0:T(8,128)(2,1)} %bitcast.44) | data formatting | bytes 16777216
  241.1 16.0 %fusion.17 = f32[1024,1024]{1,0:T(8,128)} fusion(bf16[1024,4096]{1,0:T(8,128)(2,1)} %bitcast.45), kind=kOutput, calls=%fused_computation.33 | convolution fusion | flops 8589934592 | bytes 12582912 | tf_op jit(solution)/shard_map/dot_general | solution.py:33
  257.1 0.0 all-reduce.2.cloned.1.call-update
  257.1 0.2 reduce-scatter.2.cloned.1.call-start
  257.4 15.6 %copy.22 = bf16[32,8,16,1024]{3,1,2,0:T(8,128)(2,1)} copy(bf16[32,8,16,1024]{3,2,1,0:T(8,128)(2,1)} %bitcast.41) | data formatting | bytes 16777216
  273.0 126.1 %all-reduce.2.cloned.1.call-done = f32[1024,1024]{1,0:T(8,128)} async-done(((f32[1024,1024]{1,0:T(8,128)}), f32[1024,1024]{1,0:T(8,128)}) %all-reduce.2.cloned.1.call-update) | async-done | bytes 4194320 | tf_op jit(solution)/shard_map/psum | solution.py:36
  399.1 0.0 copy-done
  399.1 2.2 convolution_convert_fusion.2
  401.3 14.5 %all_gather.6 = bf16[1024,128]{1,0:T(8,128)(2,1)S(1)} all-gather(bf16[256,128]{1,0:T(8,128)(2,1)S(1)} %convolution_convert_fusion.2), channel_id=1, replica_groups=mesh['light'=4,'pix'=4,'cam'=2] {'light'}, dimensions={0}, use_global_device_ids=true | all-gather | bytes 327680 | tf_op jit(solution)/shard_map/all_gather | solution.py:46
  415.8 0.3 fusion.18
  416.1 0.1 copy.18
  416.2 11.7 %cholesky.44 = f32[128,128]{1,0:T(8,128)S(1)} custom-call(f32[128,128]{1,0:T(8,128)S(1)} %fusion.9), custom_call_target="Cholesky" | custom-call | tf_op jit(solution)/shard_map/jit(cholesky)/cholesky | solution.py:16
  427.9 0.6 compare_reduce_fusion.1
  428.6 0.7 fusion.4
  429.3 9.8 %custom-call.6 = f32[1,128,128]{1,2,0:T(8,128)S(1)} custom-call(f32[1,128,128]{2,1,0:T(8,128)S(1)} %fusion.4), custom_call_target="InvertDiagBlocksLowerTriangular" | custom-call | tf_op jit(solution)/shard_map/triangular_solve/custom-call.0 | solution.py:17
  439.1 0.6 convolution_bitcast_fusion.1
  439.7 2.2 convolution_convert_fusion.1
  441.9 14.5 %all_gather.7 = bf16[1024,128]{1,0:T(8,128)(2,1)S(1)} all-gather(bf16[256,128]{1,0:T(8,128)(2,1)S(1)} %convolution_convert_fusion.1), channel_id=1, replica_groups=mesh['light'=4,'pix'=4,'cam'=2] {'light'}, dimensions={0}, use_global_device_ids=true | all-gather | bytes 327680 | tf_op jit(solution)/shard_map/all_gather | solution.py:46
  456.4 0.3 fusion.19
  456.7 0.1 copy.19
  456.8 11.7 %cholesky.55 = f32[128,128]{1,0:T(8,128)S(1)} custom-call(f32[128,128]{1,0:T(8,128)S(1)} %fusion.7), custom_call_target="Cholesky" | custom-call | tf_op jit(solution)/shard_map/jit(cholesky)/cholesky | solution.py:16
  468.5 0.6 compare_reduce_fusion
  469.2 0.7 fusion.5
  469.9 9.8 %custom-call.7 = f32[1,128,128]{1,2,0:T(8,128)S(1)} custom-call(f32[1,128,128]{2,1,0:T(8,128)S(1)} %fusion.5), custom_call_target="InvertDiagBlocksLowerTriangular" | custom-call | tf_op jit(solution)/shard_map/triangular_solve/custom-call.0 | solution.py:17
  479.7 0.6 convolution_bitcast_fusion
  480.3 6.6 %convolution_convert_fusion = bf16[128,16384]{1,0:T(8,128)(2,1)} fusion(bf16[256,16384]{1,0:T(8,128)(2,1)} %bitcast.42, f32[256,128]{0,1:T(8,128)S(1)} %constant_dynamic-slice_fusion), kind=kOutput, calls=%fused_computation | convolution fusion | flops 1075871744 | bytes 12713984 | tf_op jit(solution)/shard_map/dot_general | solution.py:54
  486.9 0.0 reduce-scatter.2.cloned.1.call-update
  487.0 0.8 copy.20
  487.7 75.2 %reduce-scatter.2.cloned.1.call-done = bf16[32,16384]{1,0:T(8,128)(2,1)} async-done(((bf16[128,16384]{1,0:T(8,128)(2,1)}), bf16[32,16384]{1,0:T(8,128)(2,1)}) %reduce-scatter.2.cloned.1.call-update) | async-done | bytes 1048592 | tf_op jit(solution)/shard_map/reduce_scatter | solution.py:53
  562.9 3.2 copy.23
  (5 shorter events, 0.1 us)
Async XLA Ops:
  7.2 391.9 %copy-start = (f32[1024,128]{1,0:T(8,128)S(1)}, f32[1024,128]{1,0:T(8,128)}, u32[]{:S(2)}) copy-start(f32[1024,128]{1,0:T(8,128)} %param.6) | copy-start | bytes 1572868
  7.2 391.9 %all-reduce.2.cloned.1.call-start = ((), (), s32[]{:S(2)}) async-start(), calls=%async_computation.2 | async-start | bytes 8388608 | tf_op jit(solution)/shard_map/psum | solution.py:36
  257.1 305.8 %reduce-scatter.2.cloned.1.call-start = ((), (), s32[]{:S(2)}) async-start(), calls=%async_computation.3 | async-start | bytes 5242880 | tf_op jit(solution)/shard_map/reduce_scatter | solution.py:53
Sparse Core Ops, SparseCore 0:
  257.3 141.7 all-reduce.1
  487.1 75.7 reduce-scatter.1
where the time goes:
time: 582 us; the launch traced here: 573 us
  blocking collectives  221 us (38%)
  waiting for transfers between devices  201 us (35%)
  local copies, waits for them, and re-layouts  61.5 us (11%)
  other arithmetic  45.7 us (8%)
  matrix products  28.8 us (5%)
  between operations  14.6 us (3%)
    all_to_all x1, blocking collectives, per_device(): lax.all_to_all(reflectance, 'light', split_axis=2, concat_axis=0, tiled=T...  192 us
    psum x1, waiting for transfers between devices, per_device(): full_gram = lax.psum(own_gram, ('light', 'pix', 'cam')) * inverse_cols  126 us
    reduce_scatter x1, waiting for transfers between devices, per_device(): lax.psum_scatter(lax.dot_general(rounded, fibers, (((0,), (0,)), ((), ())...  75.2 us
    unnamed x7, local copies, waits for them, and re-layouts  45.2 us
    all_gather x2, blocking collectives, per_device(): lax.all_gather(image_rows.astype(jnp.bfloat16), 'light', axis=0, tiled=True)  29 us
    another operation x6, other arithmetic, orthonormal(): factor = jnp.linalg.cholesky(inner_gram)  24.8 us
    another operation x4, other arithmetic, orthonormal(): lax.linalg.triangular_solve(factor, image_full, left_side=False, lower=Tr...  20.9 us
    all_to_all x1, local copies, waits for them, and re-layouts, per_device(): lax.all_to_all(reflectance, 'light', split_axis=2, concat_axis=0, tiled=T...  16 us
  transfers between devices with their start and end apart: 2, of which 2 were waited for; matrix products, arithmetic and copies ran while one was open for 3% of the time, Pallas kernels for 0%

commit v1 on v0

v1 whole, which is shorter than its diff:
```python
import functools

import jax
import jax.numpy as jnp
from jax import lax
from jax.experimental import pallas as pl
from jax.experimental.pallas import tpu as pltpu
from jax.sharding import PartitionSpec as P

ITERS = 2
MESH = pl.DeviceIdType.MESH


def greet(barrier, devices):
    for device in devices:
        pl.semaphore_signal(barrier, inc=1, device_id=device, device_id_type=MESH)
    pl.semaphore_wait(barrier, len(devices))


def exchange_kernel(lights, src_ref, dst_ref, bounce, local_sem, send_sem, recv_sem):
    me = lax.axis_index("light")
    peers = [lax.rem(me + step, lights) for step in range(1, lights)]
    greet(pltpu.get_barrier_semaphore(), [{"light": peer} for peer in peers])
    parts, width = src_ref.shape[1], src_ref.shape[3]
    copies = []
    for part in range(parts):
        for slot, peer in enumerate(peers):
            copy = pltpu.make_async_remote_copy(
                src_ref=src_ref.at[peer, part],
                dst_ref=dst_ref.at[me, :, pl.ds(part * width, width)],
                send_sem=send_sem.at[slot, part],
                recv_sem=recv_sem.at[slot, part],
                device_id={"light": peer},
                device_id_type=MESH,
            )
            copy.start()
            copies.append(copy)
    for part in range(parts):
        inward = pltpu.make_async_copy(src_ref.at[me, part], bounce.at[part], local_sem.at[0, part])
        inward.start()
        inward.wait()
        outward = pltpu.make_async_copy(
            bounce.at[part], dst_ref.at[me, :, pl.ds(part * width, width)], local_sem.at[1, part]
        )
        outward.start()
        outward.wait()
    for copy in copies:
        copy.wait()


def exchange(blocks, collective_id):
    lights, parts, rows, width = blocks.shape
    return pl.pallas_call(
        functools.partial(exchange_kernel, lights),
        out_shape=jax.ShapeDtypeStruct((lights, rows, parts * width), blocks.dtype),
        in_specs=[pl.BlockSpec(memory_space=pl.ANY)],
        out_specs=pl.BlockSpec(memory_space=pl.ANY),
        scratch_shapes=[
            pltpu.VMEM(blocks.shape[1:], blocks.dtype),
            pltpu.SemaphoreType.DMA((2, parts)),
            pltpu.SemaphoreType.DMA((lights - 1, parts)),
            pltpu.SemaphoreType.DMA((lights - 1, parts)),
        ],
        compiler_params=pltpu.CompilerParams(
            collective_id=collective_id, has_side_effects=True
        ),
    )(blocks)


def total_kernel(lights, pixes, cams, part_ref, out_ref, plane_buf, light_buf, own_buf,
                 send1, recv1, send2, recv2, send3, recv3):
    light = lax.axis_index("light")
    plane = pixes * cams
    me = lax.axis_index("pix") * cams + lax.axis_index("cam")
    rows = part_ref.shape[0] // plane

    def row_slice(index):
        return pl.ds(pl.multiple_of(index * rows, rows), rows)

    peers = [lax.rem(me + step, plane) for step in range(1, plane)]
    plane_devices = [{"pix": peer // cams, "cam": lax.rem(peer, cams)} for peer in peers]
    light_devices = [{"light": lax.rem(light + step, lights)} for step in range(1, lights)]
    greet(pltpu.get_barrier_semaphore(), plane_devices + light_devices)

    copies = []
    for slot, (peer, device) in enumerate(zip(peers, plane_devices)):
        copy = pltpu.make_async_remote_copy(
            src_ref=part_ref.at[row_slice(peer)],
            dst_ref=plane_buf.at[slot],
            send_sem=send1.at[slot],
            recv_sem=recv1.at[slot],
            device_id=device,
            device_id_type=MESH,
        )
        copy.start()
        copies.append(copy)
    total = part_ref[row_slice(me), :].astype(jnp.float32)
    for slot, copy in enumerate(copies):
        copy.wait_recv()
        total += plane_buf[slot].astype(jnp.float32)
    own_buf[...] = total.astype(own_buf.dtype)

    light_copies = []
    for slot, device in enumerate(light_devices):
        copy = pltpu.make_async_remote_copy(
            src_ref=own_buf,
            dst_ref=light_buf.at[light],
            send_sem=send2.at[slot],
            recv_sem=recv2.at[slot],
            device_id=device,
            device_id_type=MESH,
        )
        copy.start()
        light_copies.append(copy)
    light_buf[light] = own_buf[...]
    for copy in light_copies:
        copy.wait_recv()
    total = light_buf[0].astype(jnp.float32)
    for index in range(1, lights):
        total += light_buf[index].astype(jnp.float32)
    out_ref[row_slice(me), :] = total.astype(out_ref.dtype)

    last_copies = []
    for slot, device in enumerate(plane_devices):
        copy = pltpu.make_async_remote_copy(
            src_ref=out_ref.at[row_slice(me)],
            dst_ref=out_ref.at[row_slice(me)],
            send_sem=send3.at[slot],
            recv_sem=recv3.at[slot],
            device_id=device,
            device_id_type=MESH,
        )
        copy.start()
        last_copies.append(copy)
    for copy in copies + light_copies:
        copy.wait_send()
    for copy in last_copies:
        copy.wait()


def total_over_all(part, collective_id):
    lights, pixes, cams = (lax.axis_size(name) for name in ("light", "pix", "cam"))
    plane = pixes * cams
    rows = part.shape[0] // plane
    block = (rows, part.shape[1])
    dma = pltpu.SemaphoreType.DMA
    return pl.pallas_call(
        functools.partial(total_kernel, lights, pixes, cams),
        out_shape=jax.ShapeDtypeStruct(part.shape, part.dtype),
        in_specs=[pl.BlockSpec(memory_space=pltpu.VMEM)],
        out_specs=pl.BlockSpec(memory_space=pltpu.VMEM),
        scratch_shapes=[
            pltpu.VMEM((plane - 1,) + block, part.dtype),
            pltpu.VMEM((lights,) + block, part.dtype),
            pltpu.VMEM(block, part.dtype),
            dma((plane - 1,)), dma((plane - 1,)),
            dma((lights - 1,)), dma((lights - 1,)),
            dma((plane - 1,)), dma((plane - 1,)),
        ],
        compiler_params=pltpu.CompilerParams(
            collective_id=collective_id, has_side_effects=True
        ),
    )(part)


def orthonormal(image_full):
    inner_gram = jnp.dot(
        image_full.T,
        image_full,
        preferred_element_type=jnp.float32,
        precision=lax.Precision.HIGHEST,
    )
    factor = jnp.linalg.cholesky(inner_gram)
    return lax.linalg.triangular_solve(
        factor, image_full, left_side=False, lower=True, transpose_a=True
    )


def per_device(reflectance, start_basis):
    light_rows, camera_cols, pixels = reflectance.shape
    rank_total = start_basis.shape[1]
    light_count = lax.axis_size("light")
    position = lax.axis_index("light")
    inverse_cols = 1.0 / (camera_cols * pixels * lax.axis_size("cam") * lax.axis_size("pix"))
    own_cols = camera_cols // light_count * pixels
    blocks = reflectance.transpose(1, 0, 2).reshape(light_count, -1, light_rows, pixels)
    every_light = exchange(blocks, 0).reshape(light_rows * light_count, own_cols)

    basis_now = start_basis
    for iteration in range(ITERS):
        high = lax.reduce_precision(basis_now, 8, 7)
        pair = jnp.concatenate([high, basis_now - high], axis=1).astype(jnp.bfloat16)
        halves = lax.dot_general(
            pair, every_light, (((0,), (0,)), ((), ())), preferred_element_type=jnp.float32
        )
        projected = (halves[:rank_total] + halves[rank_total:]).astype(jnp.bfloat16)
        image_part = lax.dot_general(
            every_light, projected, (((1,), (1,)), ((), ())), preferred_element_type=jnp.float32
        )
        image_full = total_over_all((image_part * inverse_cols).astype(jnp.bfloat16), 1)
        basis_now = orthonormal(image_full.astype(jnp.float32))
    basis_rows = lax.dynamic_slice_in_dim(basis_now, position * light_rows, light_rows, 0)
    rank_rows = rank_total // light_count
    core = lax.dot_general(
        basis_now.astype(jnp.bfloat16), every_light, (((0,), (0,)), ((), ())),
        preferred_element_type=jnp.float32,
    ).astype(jnp.bfloat16)
    core_rows = exchange(core.reshape(light_count, 1, rank_rows, own_cols), 2)
    core_rows = core_rows.transpose(1, 0, 2).astype(jnp.float32)
    return (core_rows.reshape(rank_rows, camera_cols, pixels), basis_rows)


def solution(mesh):
    placed = (P("light", "cam", "pix"), P())
    return jax.shard_map(
        per_device,
        mesh=mesh,
        in_specs=placed,
        out_specs=(P("light", "cam", "pix"), P("light", None)),
        check_vma=False,
    )
```

time: 582 us -> 341 us (0.59)
  Pallas kernels: 0 us -> 244 us
  blocking collectives: 221 us -> 0 us
  waiting for transfers between devices: 201 us -> 0 us
  local copies, waits for them, and re-layouts: 61.5 us -> 15.7 us
  between operations: 14.6 us -> 0.89 us
    pallas_call x0 -> x4, Pallas kernels: none -> 244 us  [the longest x2 197 us: exchange(): pl.pallas_call(functools.partial(exchange_kernel, lights), out_shape=jax....]
    all_to_all x1 -> x0, blocking collectives: 192 us -> none  [per_device(): lax.all_to_all(reflectance, 'light', split_axis=2, concat_axis=0, tiled=T...]
    psum x1 -> x0, waiting for transfers between devices: 126 us -> none  [per_device(): full_gram = lax.psum(own_gram, ('light', 'pix', 'cam')) * inverse_cols]
    reduce_scatter x1 -> x0, waiting for transfers between devices: 75.2 us -> none  [per_device(): lax.psum_scatter(lax.dot_general(rounded, fibers, (((0,), (0,)), ((), ())...]
    unnamed x7 -> x11, local copies, waits for them, and re-layouts: 45.2 us -> 0.78 us
    all_gather x2 -> x0, blocking collectives: 29 us -> none  [per_device(): lax.all_gather(image_rows.astype(jnp.bfloat16), 'light', axis=0, tiled=True)]
    all_to_all x1 -> x0, local copies, waits for them, and re-layouts: 16 us -> none  [per_device(): lax.all_to_all(reflectance, 'light', split_axis=2, concat_axis=0, tiled=T...]
    transpose x0 -> x1, local copies, waits for them, and re-layouts: none -> 11.3 us  [per_device(): reflectance.transpose(1, 0, 2).reshape(light_count, -1, light_rows, pixels)]
  transfers between devices with their start and end apart: 2 -> 0, of which waited for: 2 -> 0; matrix products, arithmetic and copies ran while one was open for 3% -> 0% of each run, Pallas kernels for 0% -> 0%
where the time goes in v1:
time: 341 us; the launch traced here: 337 us
  Pallas kernels  244 us (72%)
  other arithmetic  47.6 us (14%)
  matrix products  29.4 us (9%)
  local copies, waits for them, and re-layouts  15.7 us (5%)
    pallas_call x2, Pallas kernels, exchange(): pl.pallas_call(functools.partial(exchange_kernel, lights), out_shape=jax....  197 us
    pallas_call x2, Pallas kernels, total_over_all(): pl.pallas_call(functools.partial(total_kernel, lights, pixes, cams), out_...  47 us
    another operation x6, other arithmetic, orthonormal(): factor = jnp.linalg.cholesky(inner_gram)  25.1 us
    another operation x4, other arithmetic, orthonormal(): lax.linalg.triangular_solve(factor, image_full, left_side=False, lower=Tr...  20.9 us
    dot_general x2, matrix products, per_device(): lax.dot_general(pair, every_light, (((0,), (0,)), ((), ())), preferred_el...  11.8 us
    transpose x1, local copies, waits for them, and re-layouts, per_device(): reflectance.transpose(1, 0, 2).reshape(light_count, -1, light_rows, pixels)  11.3 us

profile of v1, /device:TPU:0, one launch (start us, length us, event | category | flops | bytes accessed | tf_op | source)
XLA Modules:
  0.0 337.4 jit_solution(5880923750431494077)
XLA Ops:
  0.6 11.3 %copy.10 = bf16[16,256,1024]{2,1,0:T(8,128)(2,1)} copy(bf16[16,256,1024]{2,0,1:T(8,128)(2,1)} %bitcast.53) | data formatting | bytes 16777216 | tf_op jit(solution)/shard_map/transpose | solution.py:186
  11.9 0.0 copy-start
  11.9 175.2 %shard_map.41 = bf16[4,256,4096]{2,1,0:T(8,128)(2,1)} custom-call(bf16[4,4,256,1024]{3,2,1,0:T(8,128)(2,1)} %bitcast.52), custom_call_target="tpu_custom_call" | custom-call | tf_op jit(solution)/shard_map/pallas_call | solution.py:53
  187.2 0.0 copy-done
  187.2 0.0 slice-start
  187.2 0.1 reduce-precision_convert_fusion.1
  187.3 0.0 slice-start.1
  187.3 5.9 %fusion.10 = f32[256,4096]{1,0:T(8,128)S(1)} fusion(bf16[1024,4096]{1,0:T(8,128)(2,1)} %bitcast.43, bf16[1024,128]{1,0:T(8,128)(2,1)S(1)} %get-tuple-element.11, bf16[1024,128]{1,0:T(8,128)(2,1)S(1)} %get-tuple-element.10), kind=kOutput, calls=%fused_computation.20 | convolution fusion | flops 2148532224 | bytes 13107200 | tf_op jit(solution)/shard_map/dot_general | solution.py:193
  193.2 0.0 slice-done
  193.2 0.0 slice-done.1
  193.3 3.0 fusion.5.part_ref
  196.3 28.7 %shard_map.42 = bf16[1024,128]{1,0:T(8,128)(2,1)} custom-call(bf16[1024,128]{1,0:T(8,128)(2,1)} %fusion.5.part_ref), custom_call_target="tpu_custom_call" | custom-call | tf_op jit(solution)/shard_map/pallas_call | solution.py:147
  225.0 1.3 fusion.31
  226.3 0.1 copy.12
  226.4 11.8 %cholesky.44 = f32[128,128]{1,0:T(8,128)S(1)} custom-call(f32[128,128]{1,0:T(8,128)S(1)} %fusion.26), custom_call_target="Cholesky" | custom-call | tf_op jit(solution)/shard_map/jit(cholesky)/cholesky | solution.py:173
  238.3 0.6 compare_reduce_fusion.1
  238.9 0.7 fusion.21
  239.6 9.8 %custom-call.6 = f32[1,128,128]{1,2,0:T(8,128)S(1)} custom-call(f32[1,128,128]{2,1,0:T(8,128)S(1)} %fusion.21), custom_call_target="InvertDiagBlocksLowerTriangular" | custom-call | tf_op jit(solution)/shard_map/triangular_solve/custom-call.0 | solution.py:174
  249.4 0.0 slice-start.2
  249.4 1.7 reduce-precision_convert_fusion
  251.1 0.0 slice-start.3
  251.1 5.9 %fusion.14 = f32[256,4096]{1,0:T(8,128)S(1)} fusion(bf16[1024,4096]{1,0:T(8,128)(2,1)} %bitcast.44, bf16[1024,128]{0,1:T(8,128)(2,1)S(1)} %get-tuple-element.9, bf16[1024,128]{0,1:T(8,128)(2,1)S(1)} %get-tuple-element.8), kind=kOutput, calls=%fused_computation.24 | convolution fusion | flops 2148532224 | bytes 13107200 | tf_op jit(solution)/shard_map/dot_general | solution.py:193
  257.0 0.0 slice-done.2
  257.0 0.0 slice-done.3
  257.1 3.0 fusion.4.part_ref
  260.1 18.3 %shard_map.43 = bf16[1024,128]{1,0:T(8,128)(2,1)} custom-call(bf16[1024,128]{1,0:T(8,128)(2,1)} %fusion.4.part_ref), custom_call_target="tpu_custom_call" | custom-call | tf_op jit(solution)/shard_map/pallas_call | solution.py:147
  278.4 1.3 fusion.32
  279.7 0.1 copy.14
  279.8 11.9 %cholesky.55 = f32[128,128]{1,0:T(8,128)S(1)} custom-call(f32[128,128]{1,0:T(8,128)S(1)} %fusion.24), custom_call_target="Cholesky" | custom-call | tf_op jit(solution)/shard_map/jit(cholesky)/cholesky | solution.py:173
  291.7 0.6 compare_reduce_fusion
  292.4 0.7 fusion.22
  293.1 9.8 %custom-call.7 = f32[1,128,128]{1,2,0:T(8,128)S(1)} custom-call(f32[1,128,128]{2,1,0:T(8,128)S(1)} %fusion.22), custom_call_target="InvertDiagBlocksLowerTriangular" | custom-call | tf_op jit(solution)/shard_map/triangular_solve/custom-call.0 | solution.py:174
  302.9 1.6 convolution_bitcast_fusion
  304.5 5.6 %convolution_convert_fusion = bf16[128,4096]{1,0:T(8,128)(2,1)} fusion(bf16[1024,4096]{1,0:T(8,128)(2,1)} %bitcast.45, f32[1024,128]{0,1:T(8,128)S(1)} %convolution_bitcast_fusion), kind=kOutput, calls=%fused_computation | convolution fusion | flops 1074397184 | bytes 9961472 | tf_op jit(solution)/shard_map/dot_general | solution.py:204
  310.1 21.7 %shard_map.44 = bf16[4,32,4096]{2,1,0:T(8,128)(2,1)} custom-call(bf16[4,1,32,4096]{3,2,1,0:T(8,128)(2,1)} %bitcast.54), custom_call_target="tpu_custom_call" | custom-call | tf_op jit(solution)/shard_map/pallas_call | solution.py:53
  331.8 1.4 convert_bitcast_fusion
  333.2 1.4 copy.15
  334.5 2.1 reshape.38
  336.6 0.8 copy.16
  (7 shorter events, 0.1 us)
Async XLA Ops:
  11.9 175.3 %copy-start = (f32[1024,128]{1,0:T(8,128)S(1)}, f32[1024,128]{1,0:T(8,128)}, u32[]{:S(2)}) copy-start(f32[1024,128]{1,0:T(8,128)} %param.6) | copy-start | bytes 1572868
  187.2 6.0 %slice-start = ((s8[8388608]{0:T(1024)(128)(4,1)}), s8[4194304]{0:T(1024)(128)(4,1)S(1)}, s32[]{:S(2)}) async-start(s8[8388608]{0:T(1024)(128)(4,1)} %bitcast.46), calls=%async_computation | async-start | bytes 8388608
  187.3 5.9 %slice-start.1 = ((s8[8388608]{0:T(1024)(128)(4,1)}), s8[4194304]{0:T(1024)(128)(4,1)S(1)}, s32[]{:S(2)}) async-start(s8[8388608]{0:T(1024)(128)(4,1)} %bitcast.46), calls=%async_computation.1 | async-start | bytes 8388608
  249.4 7.6 %slice-start.2 = ((s8[8388608]{0:T(1024)(128)(4,1)}), s8[4194304]{0:T(1024)(128)(4,1)S(1)}, s32[]{:S(2)}) async-start(s8[8388608]{0:T(1024)(128)(4,1)} %bitcast.49), calls=%async_computation.2 | async-start | bytes 8388608
  251.1 5.9 %slice-start.3 = ((s8[8388608]{0:T(1024)(128)(4,1)}), s8[4194304]{0:T(1024)(128)(4,1)S(1)}, s32[]{:S(2)}) async-start(s8[8388608]{0:T(1024)(128)(4,1)} %bitcast.49), calls=%async_computation.3 | async-start | bytes 8388608

commit v2 on v1

--- a/solution.py
+++ b/solution.py
@@ -163,17 +163,85 @@
     )(part)
 
 
-def orthonormal(image_full):
-    inner_gram = jnp.dot(
-        image_full.T,
-        image_full,
-        preferred_element_type=jnp.float32,
-        precision=lax.Precision.HIGHEST,
-    )
-    factor = jnp.linalg.cholesky(inner_gram)
-    return lax.linalg.triangular_solve(
-        factor, image_full, left_side=False, lower=True, transpose_a=True
-    )
+def orthonormal_kernel(image_ref, basis_ref, pair_ref):
+    image = image_ref[...]
+    rank = image.shape[1]
+    inner = lax.dot_general(image, image, (((0,), (0,)), ((), ())), preferred_element_type=jnp.float32)
+    height = 8
+    shape = (height, rank)
+    sub = lax.broadcasted_iota(jnp.int32, shape, 0)
+    lane = lax.broadcasted_iota(jnp.int32, shape, 1)
+    count = rank // height
+    left = [inner[height * t : height * (t + 1), :] for t in range(count)]
+    right = [jnp.where(lane == sub + height * t, 1.0, 0.0) for t in range(count)]
+
+    def spread_row(tile, k):
+        return jnp.broadcast_to(tile[k : k + 1, :], shape)
+
+    def spread_column(tile, j):
+        return jnp.broadcast_to(tile[:, j : j + 1], shape)
+
+    for p in range(count):
+        first = height * p
+        top, below = left[p], right[p]
+        columns = [spread_column(top, first + k) for k in range(height)]
+        inverses, pivots = [], jnp.ones(shape, jnp.float32)
+        for k in range(height):
+            pivot = spread_row(columns[k], k)
+            inverse = 1.0 / pivot
+            pivots = jnp.where(sub == k, pivot, pivots)
+            inverses.append(inverse)
+            factor = jnp.where(sub > k, columns[k] * inverse, 0.0)
+            for later in range(k + 1, height):
+                columns[later] = columns[later] - factor * spread_row(columns[later], k)
+            top = top - factor * spread_row(top, k)
+            below = below - factor * spread_row(below, k)
+        right[p] = below * lax.rsqrt(pivots)
+        top_rows = [spread_row(top, k) * inverses[k] for k in range(height)]
+        below_rows = [spread_row(below, k) * inverses[k] for k in range(height)]
+        steps = [
+            [spread_row(columns[later], k) * inverses[k] for later in range(k + 1, height)]
+            for k in range(height)
+        ]
+        for t in range(p + 1, count):
+            own = [spread_column(left[t], first + k) for k in range(height)]
+            upper, lower = left[t], right[t]
+            for k in range(height):
+                for index, later in enumerate(range(k + 1, height)):
+                    own[later] = own[later] - own[k] * steps[k][index]
+                upper = upper - own[k] * top_rows[k]
+                lower = lower - own[k] * below_rows[k]
+            left[t], right[t] = upper, lower
+    inverse = jnp.concatenate(right, axis=0)
+    pieces = []
+    for _ in range(3):
+        piece = inverse.astype(jnp.bfloat16)
+        pieces.append(piece)
+        inverse = inverse - piece.astype(jnp.float32)
+    basis = None
+    for piece in reversed(pieces):
+        term = lax.dot_general(
+            image, piece, (((1,), (1,)), ((), ())), preferred_element_type=jnp.float32
+        )
+        basis = term if basis is None else basis + term
+    basis_ref[...] = basis
+    high = basis.astype(jnp.bfloat16)
+    pair_ref[:, :rank] = high
+    pair_ref[:, rank:] = (basis - high.astype(jnp.float32)).astype(jnp.bfloat16)
+
+
+def orthonormal(image):
+    rows, rank = image.shape
+    vmem = pl.BlockSpec(memory_space=pltpu.VMEM)
+    return pl.pallas_call(
+        orthonormal_kernel,
+        out_shape=(
+            jax.ShapeDtypeStruct((rows, rank), jnp.float32),
+            jax.ShapeDtypeStruct((rows, 2 * rank), jnp.bfloat16),
+        ),
+        in_specs=[vmem],
+        out_specs=(vmem, vmem),
+    )(image)
 
 
 def per_device(reflectance, start_basis):
@@ -186,10 +254,9 @@
     blocks = reflectance.transpose(1, 0, 2).reshape(light_count, -1, light_rows, pixels)
     every_light = exchange(blocks, 0).reshape(light_rows * light_count, own_cols)
 
-    basis_now = start_basis
+    high = lax.reduce_precision(start_basis, 8, 7)
+    pair = jnp.concatenate([high, start_basis - high], axis=1).astype(jnp.bfloat16)
     for iteration in range(ITERS):
-        high = lax.reduce_precision(basis_now, 8, 7)
-        pair = jnp.concatenate([high, basis_now - high], axis=1).astype(jnp.bfloat16)
         halves = lax.dot_general(
             pair, every_light, (((0,), (0,)), ((), ())), preferred_element_type=jnp.float32
         )
@@ -198,11 +265,11 @@
             every_light, projected, (((1,), (1,)), ((), ())), preferred_element_type=jnp.float32
         )
         image_full = total_over_all((image_part * inverse_cols).astype(jnp.bfloat16), 1)
-        basis_now = orthonormal(image_full.astype(jnp.float32))
+        basis_now, pair = orthonormal(image_full)
     basis_rows = lax.dynamic_slice_in_dim(basis_now, position * light_rows, light_rows, 0)
     rank_rows = rank_total // light_count
     core = lax.dot_general(
-        basis_now.astype(jnp.bfloat16), every_light, (((0,), (0,)), ((), ())),
+        pair[:, :rank_total], every_light, (((0,), (0,)), ((), ())),
         preferred_element_type=jnp.float32,
     ).astype(jnp.bfloat16)
     core_rows = exchange(core.reshape(light_count, 1, rank_rows, own_cols), 2)

time: 341 us -> 307 us (0.900)
  other arithmetic: 47.6 us -> 1.51 us
  Pallas kernels: 244 us -> 258 us
    another operation x11 -> x1, other arithmetic: 46.1 us -> 0.09 us  [the longest x6 25.1 us: orthonormal(): factor = jnp.linalg.cholesky(inner_gram)]
    pallas_call x0 -> x2, Pallas kernels: none -> 14.4 us  [orthonormal(): pl.pallas_call(orthonormal_kernel, out_shape=(jax.ShapeDtypeStruct((rows,...]
    dot_general x3 -> x1, matrix products: 8.21 us -> 5.73 us  [per_device(): lax.dot_general(pair[:, :rank_total], every_light, (((0,), (0,)), ((), ()...]
where the time goes in v2:
time: 307 us; the launch traced here: 304 us
  Pallas kernels  258 us (84%)
  matrix products  27.1 us (9%)
  local copies, waits for them, and re-layouts  16.3 us (5%)
    pallas_call x2, Pallas kernels, exchange(): pl.pallas_call(functools.partial(exchange_kernel, lights), out_shape=jax....  197 us
    pallas_call x2, Pallas kernels, total_over_all(): pl.pallas_call(functools.partial(total_kernel, lights, pixes, cams), out_...  47 us
    pallas_call x2, Pallas kernels, orthonormal(): pl.pallas_call(orthonormal_kernel, out_shape=(jax.ShapeDtypeStruct((rows,...  14.4 us
    dot_general x2, matrix products, per_device(): lax.dot_general(pair, every_light, (((0,), (0,)), ((), ())), preferred_el...  11.9 us
    transpose x1, local copies, waits for them, and re-layouts, per_device(): reflectance.transpose(1, 0, 2).reshape(light_count, -1, light_rows, pixels)  11.3 us
    dot_general x2, matrix products, per_device(): lax.dot_general(every_light, projected, (((1,), (1,)), ((), ())), preferr...  9.47 us

profile of v2, /device:TPU:0, one launch (start us, length us, event | category | flops | bytes accessed | tf_op | source)
XLA Modules:
  0.0 304.0 jit_solution(1132740478224396842)
XLA Ops:
  0.6 11.3 %copy.6 = bf16[16,256,1024]{2,1,0:T(8,128)(2,1)} copy(bf16[16,256,1024]{2,0,1:T(8,128)(2,1)} %bitcast.24) | data formatting | bytes 16777216 | tf_op jit(solution)/shard_map/transpose | solution.py:254
  11.9 0.0 copy-start
  11.9 175.2 %shard_map.41 = bf16[4,256,4096]{2,1,0:T(8,128)(2,1)} custom-call(bf16[4,4,256,1024]{3,2,1,0:T(8,128)(2,1)} %bitcast.23), custom_call_target="tpu_custom_call" | custom-call | tf_op jit(solution)/shard_map/pallas_call | solution.py:53
  187.2 0.0 copy-done
  187.2 0.0 slice-start
  187.2 0.1 reduce-precision_convert_fusion
  187.3 0.0 slice-start.1
  187.3 5.9 %fusion.9 = f32[256,4096]{1,0:T(8,128)S(1)} fusion(bf16[1024,4096]{1,0:T(8,128)(2,1)} %bitcast.16, bf16[1024,128]{1,0:T(8,128)(2,1)S(1)} %get-tuple-element.9, bf16[1024,128]{1,0:T(8,128)(2,1)S(1)} %get-tuple-element.8), kind=kOutput, calls=%fused_computation.15 | convolution fusion | flops 2148532224 | bytes 13107200 | tf_op jit(solution)/shard_map/dot_general | solution.py:260
  193.2 0.0 slice-done
  193.3 0.0 slice-done.1
  193.3 3.0 fusion.5.part_ref
  196.3 28.7 %shard_map.42.image_ref = bf16[1024,128]{1,0:T(8,128)(2,1)} custom-call(bf16[1024,128]{1,0:T(8,128)(2,1)} %fusion.5.part_ref), custom_call_target="tpu_custom_call" | custom-call | tf_op jit(solution)/shard_map/pallas_call | solution.py:147
  225.0 7.3 %shard_map.43 = (f32[1024,128]{1,0:T(8,128)}, bf16[1024,256]{1,0:T(8,128)(2,1)}) custom-call(bf16[1024,128]{1,0:T(8,128)(2,1)} %shard_map.42.image_ref), custom_call_target="tpu_custom_call" | custom-call | tf_op jit(solution)/shard_map/pallas_call | solution.py:236
  232.3 5.9 %fusion.15 = f32[256,4096]{1,0:T(8,128)S(1)} fusion(bf16[1024,256]{1,0:T(8,128)(2,1)} %get-tuple-element.5, bf16[1024,4096]{1,0:T(8,128)(2,1)} %bitcast.17), kind=kOutput, calls=%fused_computation.22 | convolution fusion | flops 2147483648 | bytes 13107200 | tf_op jit(solution)/shard_map/dot_general | solution.py:260
  238.3 6.4 %fusion.4.part_ref = bf16[1024,128]{1,0:T(8,128)(2,1)} fusion(bf16[1024,4096]{1,0:T(8,128)(2,1)} %bitcast.18, f32[256,4096]{1,0:T(8,128)S(1)} %fusion.15), kind=kOutput, calls=%fused_computation.10 | convolution fusion | flops 1075052544 | bytes 12845056 | tf_op jit(solution)/shard_map/dot_general | solution.py:264
  244.7 18.3 %shard_map.44.image_ref = bf16[1024,128]{1,0:T(8,128)(2,1)} custom-call(bf16[1024,128]{1,0:T(8,128)(2,1)} %fusion.4.part_ref), custom_call_target="tpu_custom_call" | custom-call | tf_op jit(solution)/shard_map/pallas_call | solution.py:147
  263.0 7.1 %shard_map.45 = (f32[1024,128]{1,0:T(8,128)}, bf16[1024,256]{1,0:T(8,128)(2,1)}) custom-call(bf16[1024,128]{1,0:T(8,128)(2,1)} %shard_map.44.image_ref), custom_call_target="tpu_custom_call" | custom-call | tf_op jit(solution)/shard_map/pallas_call | solution.py:236
  270.2 1.6 constant_dynamic-slice_fusion
  271.7 5.7 %convolution_convert_fusion = bf16[128,4096]{1,0:T(8,128)(2,1)} fusion(bf16[1024,4096]{1,0:T(8,128)(2,1)} %bitcast.19, bf16[1024,256]{1,0:T(8,128)(2,1)} %get-tuple-element.6), kind=kOutput, calls=%fused_computation | convolution fusion | flops 1074266112 | bytes 9699328 | tf_op jit(solution)/shard_map/dot_general | solution.py:271
  277.5 21.7 %shard_map.46 = bf16[4,32,4096]{2,1,0:T(8,128)(2,1)} custom-call(bf16[4,1,32,4096]{3,2,1,0:T(8,128)(2,1)} %bitcast.25), custom_call_target="tpu_custom_call" | custom-call | tf_op jit(solution)/shard_map/pallas_call | solution.py:53
  299.2 1.4 convert_bitcast_fusion
  300.6 1.4 copy.8
  301.9 2.1 reshape.25
  (1 shorter events, 0.0 us)
Async XLA Ops:
  11.9 175.3 %copy-start = (f32[1024,128]{1,0:T(8,128)S(1)}, f32[1024,128]{1,0:T(8,128)}, u32[]{:S(2)}) copy-start(f32[1024,128]{1,0:T(8,128)} %param.3) | copy-start | bytes 1572868
  187.2 6.0 %slice-start = ((s8[8388608]{0:T(1024)(128)(4,1)}), s8[4194304]{0:T(1024)(128)(4,1)S(1)}, s32[]{:S(2)}) async-start(s8[8388608]{0:T(1024)(128)(4,1)} %bitcast.20), calls=%async_computation | async-start | bytes 8388608
  187.3 5.9 %slice-start.1 = ((s8[8388608]{0:T(1024)(128)(4,1)}), s8[4194304]{0:T(1024)(128)(4,1)S(1)}, s32[]{:S(2)}) async-start(s8[8388608]{0:T(1024)(128)(4,1)} %bitcast.20), calls=%async_computation.1 | async-start | bytes 8388608

commit v3 on v2

--- a/solution.py
+++ b/solution.py
@@ -19,22 +19,38 @@
 
 def exchange_kernel(lights, src_ref, dst_ref, bounce, local_sem, send_sem, recv_sem):
     me = lax.axis_index("light")
-    peers = [lax.rem(me + step, lights) for step in range(1, lights)]
-    greet(pltpu.get_barrier_semaphore(), [{"light": peer} for peer in peers])
+    barrier = pltpu.get_barrier_semaphore()
+    greet(barrier, [{"light": lax.rem(me + step, lights)} for step in range(1, lights)])
     parts, width = src_ref.shape[1], src_ref.shape[3]
-    copies = []
-    for part in range(parts):
-        for slot, peer in enumerate(peers):
-            copy = pltpu.make_async_remote_copy(
-                src_ref=src_ref.at[peer, part],
-                dst_ref=dst_ref.at[me, :, pl.ds(part * width, width)],
-                send_sem=send_sem.at[slot, part],
-                recv_sem=recv_sem.at[slot, part],
-                device_id={"light": peer},
-                device_id_type=MESH,
-            )
-            copy.start()
-            copies.append(copy)
+
+    def both_ways(action):
+        for distance in range(1, lights):
+            for side in range(2):
+                peer = me + distance if side == 0 else me - distance
+                inside = peer < lights if side == 0 else peer >= 0
+                pl.when(inside)(functools.partial(action, peer, 2 * (distance - 1) + side))
+
+    def copy_of(peer, slot, part):
+        return pltpu.make_async_remote_copy(
+            src_ref=src_ref.at[peer, part],
+            dst_ref=dst_ref.at[me, :, pl.ds(part * width, width)],
+            send_sem=send_sem.at[slot, part],
+            recv_sem=recv_sem.at[slot, part],
+            device_id={"light": peer},
+            device_id_type=MESH,
+        )
+
+    def start(peer, slot):
+        for part in range(parts):
+            copy_of(peer, slot, part).start()
+
+    def finish(peer, slot):
+        opposite = slot + 1 - 2 * (slot % 2)
+        for part in range(parts):
+            copy_of(peer, slot, part).wait_send()
+            copy_of(peer, opposite, part).wait_recv()
+
+    both_ways(start)
     for part in range(parts):
         inward = pltpu.make_async_copy(src_ref.at[me, part], bounce.at[part], local_sem.at[0, part])
         inward.start()
@@ -44,8 +60,7 @@
         )
         outward.start()
         outward.wait()
-    for copy in copies:
-        copy.wait()
+    both_ways(finish)
 
 
 def exchange(blocks, collective_id):
@@ -58,8 +73,8 @@
         scratch_shapes=[
             pltpu.VMEM(blocks.shape[1:], blocks.dtype),
             pltpu.SemaphoreType.DMA((2, parts)),
-            pltpu.SemaphoreType.DMA((lights - 1, parts)),
-            pltpu.SemaphoreType.DMA((lights - 1, parts)),
+            pltpu.SemaphoreType.DMA((2 * (lights - 1), parts)),
+            pltpu.SemaphoreType.DMA((2 * (lights - 1), parts)),
         ],
         compiler_params=pltpu.CompilerParams(
             collective_id=collective_id, has_side_effects=True
@@ -163,7 +178,7 @@
     )(part)
 
 
-def orthonormal_kernel(image_ref, basis_ref, pair_ref):
+def orthonormal_kernel(image_ref, basis_ref, pair_ref, whole):
     image = image_ref[...]
     rank = image.shape[1]
     inner = lax.dot_general(image, image, (((0,), (0,)), ((), ())), preferred_element_type=jnp.float32)
@@ -224,7 +239,9 @@
             image, piece, (((1,), (1,)), ((), ())), preferred_element_type=jnp.float32
         )
         basis = term if basis is None else basis + term
-    basis_ref[...] = basis
+    whole[...] = basis
+    own = basis_ref.shape[0]
+    basis_ref[...] = whole[pl.ds(pl.multiple_of(lax.axis_index("light") * own, own), own), :]
     high = basis.astype(jnp.bfloat16)
     pair_ref[:, :rank] = high
     pair_ref[:, rank:] = (basis - high.astype(jnp.float32)).astype(jnp.bfloat16)
@@ -232,15 +249,17 @@
 
 def orthonormal(image):
     rows, rank = image.shape
+    own = rows // lax.axis_size("light")
     vmem = pl.BlockSpec(memory_space=pltpu.VMEM)
     return pl.pallas_call(
         orthonormal_kernel,
         out_shape=(
-            jax.ShapeDtypeStruct((rows, rank), jnp.float32),
+            jax.ShapeDtypeStruct((own, rank), jnp.float32),
             jax.ShapeDtypeStruct((rows, 2 * rank), jnp.bfloat16),
         ),
         in_specs=[vmem],
         out_specs=(vmem, vmem),
+        scratch_shapes=[pltpu.VMEM((rows, rank), jnp.float32)],
     )(image)
 
 
@@ -248,7 +267,6 @@
     light_rows, camera_cols, pixels = reflectance.shape
     rank_total = start_basis.shape[1]
     light_count = lax.axis_size("light")
-    position = lax.axis_index("light")
     inverse_cols = 1.0 / (camera_cols * pixels * lax.axis_size("cam") * lax.axis_size("pix"))
     own_cols = camera_cols // light_count * pixels
     blocks = reflectance.transpose(1, 0, 2).reshape(light_count, -1, light_rows, pixels)
@@ -265,8 +283,7 @@
             every_light, projected, (((1,), (1,)), ((), ())), preferred_element_type=jnp.float32
         )
         image_full = total_over_all((image_part * inverse_cols).astype(jnp.bfloat16), 1)
-        basis_now, pair = orthonormal(image_full)
-    basis_rows = lax.dynamic_slice_in_dim(basis_now, position * light_rows, light_rows, 0)
+        basis_rows, pair = orthonormal(image_full)
     rank_rows = rank_total // light_count
     core = lax.dot_general(
         pair[:, :rank_total], every_light, (((0,), (0,)), ((), ())),

time: 307 us -> 308 us (level)
  Pallas kernels: 258 us -> 263 us
    pallas_call x2, Pallas kernels: 197 us -> 214 us  [exchange(): pl.pallas_call(functools.partial(exchange_kernel, lights), out_shape=jax....]
    pallas_call x2, Pallas kernels: 47 us -> 34.9 us  [total_over_all(): pl.pallas_call(functools.partial(total_kernel, lights, pixes, cams), out_...]
where the time goes in v3:
time: 308 us; the launch traced here: 307 us
  Pallas kernels  263 us (85%)
  matrix products  27.1 us (9%)
  local copies, waits for them, and re-layouts  14.8 us (5%)
    pallas_call x2, Pallas kernels, exchange(): pl.pallas_call(functools.partial(exchange_kernel, lights), out_shape=jax....  214 us
    pallas_call x2, Pallas kernels, total_over_all(): pl.pallas_call(functools.partial(total_kernel, lights, pixes, cams), out_...  34.9 us
    pallas_call x2, Pallas kernels, orthonormal(): pl.pallas_call(orthonormal_kernel, out_shape=(jax.ShapeDtypeStruct((own,...  14.2 us
    dot_general x2, matrix products, per_device(): lax.dot_general(pair, every_light, (((0,), (0,)), ((), ())), preferred_el...  11.9 us
    transpose x1, local copies, waits for them, and re-layouts, per_device(): reflectance.transpose(1, 0, 2).reshape(light_count, -1, light_rows, pixels)  11.3 us
    dot_general x2, matrix products, per_device(): lax.dot_general(every_light, projected, (((1,), (1,)), ((), ())), preferr...  9.46 us

profile of v3, /device:TPU:0, one launch (start us, length us, event | category | flops | bytes accessed | tf_op | source)
XLA Modules:
  0.0 307.5 jit_solution(12978226417537931149)
XLA Ops:
  0.6 11.3 %copy.6 = bf16[16,256,1024]{2,1,0:T(8,128)(2,1)} copy(bf16[16,256,1024]{2,0,1:T(8,128)(2,1)} %bitcast.24) | data formatting | bytes 16777216 | tf_op jit(solution)/shard_map/transpose | solution.py:272
  11.9 0.0 copy-start
  11.9 186.6 %shard_map.41 = bf16[4,256,4096]{2,1,0:T(8,128)(2,1)} custom-call(bf16[4,4,256,1024]{3,2,1,0:T(8,128)(2,1)} %bitcast.23), custom_call_target="tpu_custom_call" | custom-call | tf_op jit(solution)/shard_map/pallas_call | solution.py:68
  198.6 0.0 copy-done
  198.6 0.0 slice-start
  198.6 0.1 reduce-precision_convert_fusion
  198.7 0.0 slice-start.1
  198.7 5.9 %fusion.9 = f32[256,4096]{1,0:T(8,128)S(1)} fusion(bf16[1024,4096]{1,0:T(8,128)(2,1)} %bitcast.16, bf16[1024,128]{1,0:T(8,128)(2,1)S(1)} %get-tuple-element.9, bf16[1024,128]{1,0:T(8,128)(2,1)S(1)} %get-tuple-element.8), kind=kOutput, calls=%fused_computation.15 | convolution fusion | flops 2148532224 | bytes 13107200 | tf_op jit(solution)/shard_map/dot_general | solution.py:278
  204.6 0.0 slice-done
  204.6 0.0 slice-done.1
  204.7 3.0 fusion.5.part_ref
  207.7 17.4 %shard_map.42.image_ref = bf16[1024,128]{1,0:T(8,128)(2,1)} custom-call(bf16[1024,128]{1,0:T(8,128)(2,1)} %fusion.5.part_ref), custom_call_target="tpu_custom_call" | custom-call | tf_op jit(solution)/shard_map/pallas_call | solution.py:162
  225.1 7.2 %shard_map.43 = (f32[256,128]{1,0:T(8,128)}, bf16[1024,256]{1,0:T(8,128)(2,1)}) custom-call(bf16[1024,128]{1,0:T(8,128)(2,1)} %shard_map.42.image_ref), custom_call_target="tpu_custom_call" | custom-call | tf_op jit(solution)/shard_map/pallas_call | solution.py:254
  232.3 5.9 %fusion.15 = f32[256,4096]{1,0:T(8,128)S(1)} fusion(bf16[1024,256]{1,0:T(8,128)(2,1)} %get-tuple-element.5, bf16[1024,4096]{1,0:T(8,128)(2,1)} %bitcast.17), kind=kOutput, calls=%fused_computation.21 | convolution fusion | flops 2147483648 | bytes 13107200 | tf_op jit(solution)/shard_map/dot_general | solution.py:278
  238.2 6.4 %fusion.4.part_ref = bf16[1024,128]{1,0:T(8,128)(2,1)} fusion(bf16[1024,4096]{1,0:T(8,128)(2,1)} %bitcast.18, f32[256,4096]{1,0:T(8,128)S(1)} %fusion.15), kind=kOutput, calls=%fused_computation.10 | convolution fusion | flops 1075052544 | bytes 12845056 | tf_op jit(solution)/shard_map/dot_general | solution.py:282
  244.7 17.5 %shard_map.44.image_ref = bf16[1024,128]{1,0:T(8,128)(2,1)} custom-call(bf16[1024,128]{1,0:T(8,128)(2,1)} %fusion.4.part_ref), custom_call_target="tpu_custom_call" | custom-call | tf_op jit(solution)/shard_map/pallas_call | solution.py:162
  262.2 7.0 %shard_map.45 = (f32[256,128]{1,0:T(8,128)}, bf16[1024,256]{1,0:T(8,128)(2,1)}) custom-call(bf16[1024,128]{1,0:T(8,128)(2,1)} %shard_map.44.image_ref), custom_call_target="tpu_custom_call" | custom-call | tf_op jit(solution)/shard_map/pallas_call | solution.py:254
  269.2 5.7 %convolution_convert_fusion = bf16[128,4096]{1,0:T(8,128)(2,1)} fusion(bf16[1024,4096]{1,0:T(8,128)(2,1)} %bitcast.19, bf16[1024,256]{1,0:T(8,128)(2,1)} %get-tuple-element.6), kind=kOutput, calls=%fused_computation | convolution fusion | flops 1074266112 | bytes 9699328 | tf_op jit(solution)/shard_map/dot_general | solution.py:288
  274.9 27.6 %shard_map.46 = bf16[4,32,4096]{2,1,0:T(8,128)(2,1)} custom-call(bf16[4,1,32,4096]{3,2,1,0:T(8,128)(2,1)} %bitcast.25), custom_call_target="tpu_custom_call" | custom-call | tf_op jit(solution)/shard_map/pallas_call | solution.py:68
  302.6 1.4 convert_bitcast_fusion
  304.0 1.4 copy.8
  305.4 2.1 reshape.25
  (1 shorter events, 0.0 us)
Async XLA Ops:
  11.9 186.7 %copy-start = (f32[1024,128]{1,0:T(8,128)S(1)}, f32[1024,128]{1,0:T(8,128)}, u32[]{:S(2)}) copy-start(f32[1024,128]{1,0:T(8,128)} %param.3) | copy-start | bytes 1572868
  198.6 6.0 %slice-start = ((s8[8388608]{0:T(1024)(128)(4,1)}), s8[4194304]{0:T(1024)(128)(4,1)S(1)}, s32[]{:S(2)}) async-start(s8[8388608]{0:T(1024)(128)(4,1)} %bitcast.20), calls=%async_computation | async-start | bytes 8388608
  198.7 5.9 %slice-start.1 = ((s8[8388608]{0:T(1024)(128)(4,1)}), s8[4194304]{0:T(1024)(128)(4,1)S(1)}, s32[]{:S(2)}) async-start(s8[8388608]{0:T(1024)(128)(4,1)} %bitcast.20), calls=%async_computation.1 | async-start | bytes 8388608

commit v4 on v2

--- a/solution.py
+++ b/solution.py
@@ -15,6 +15,142 @@
     for device in devices:
         pl.semaphore_signal(barrier, inc=1, device_id=device, device_id_type=MESH)
     pl.semaphore_wait(barrier, len(devices))
+
+
+def gather_kernel(lights, blocks, scale, source_ref, pair_ref, every_ref, image_ref, arrived, turned, tile, left, total,
+                  load_sem, own_sem, tile_sem, send_sem, recv_sem, first_send, first_recv):
+    me = lax.axis_index("light")
+    rows, cams, width = source_ref.shape
+    parts = cams // lights
+    rank = image_ref.shape[1]
+    height = rows // blocks
+    step_rows = 16
+    peers = [lax.rem(me + step, lights) for step in range(1, lights)]
+
+    def load(block):
+        return pltpu.make_async_copy(
+            source_ref.at[pl.ds(block * height, height)], arrived.at[block % 2], load_sem.at[block % 2]
+        )
+
+    load(0).start()
+    greet(pltpu.get_barrier_semaphore(), [{"light": peer} for peer in peers])
+
+    def columns(part):
+        return pl.ds(part * width, width)
+
+    def first_copy(slot, peer, block):
+        span = pl.ds(block * height, height)
+        return pltpu.make_async_remote_copy(
+            src_ref=turned.at[peer * parts, span],
+            dst_ref=every_ref.at[me, span, columns(0)],
+            send_sem=first_send.at[slot, block],
+            recv_sem=first_recv.at[slot, block],
+            device_id={"light": peer},
+            device_id_type=MESH,
+        )
+
+    def later_copy(slot, peer, part):
+        return pltpu.make_async_remote_copy(
+            src_ref=turned.at[peer * parts + part],
+            dst_ref=every_ref.at[me, :, columns(part)],
+            send_sem=send_sem.at[slot, part],
+            recv_sem=recv_sem.at[slot, part],
+            device_id={"light": peer},
+            device_id_type=MESH,
+        )
+
+    copies = [[] for _ in range(parts)]
+    for block in range(blocks):
+        if block + 1 < blocks:
+            load(block + 1).start()
+        load(block).wait()
+
+        def turn(index, carry):
+            start = pl.multiple_of(index * step_rows, step_rows)
+            turned[:, pl.ds(pl.multiple_of(block * height + start, step_rows), step_rows), :] = jnp.transpose(
+                arrived[block % 2, pl.ds(start, step_rows)], (1, 0, 2)
+            )
+            return carry
+
+        lax.fori_loop(0, height // step_rows, turn, 0)
+        for slot, peer in enumerate(peers):
+            copies[0].append(first_copy(slot, peer, block))
+            copies[0][-1].start()
+    for part in range(1, parts):
+        for slot, peer in enumerate(peers):
+            copies[part].append(later_copy(slot, peer, part))
+            copies[part][-1].start()
+    own = [
+        pltpu.make_async_copy(turned.at[me * parts + part], every_ref.at[me, :, columns(part)], own_sem.at[part])
+        for part in range(parts)
+    ]
+    for copy in own:
+        copy.start()
+
+    left[...] = pair_ref[...].T
+    total[...] = jnp.zeros_like(total)
+    chunk = 256
+    for part in range(parts):
+        own[part].wait()
+        for copy in copies[part]:
+            copy.wait_recv()
+        reads = [
+            pltpu.make_async_copy(
+                every_ref.at[light, :, columns(part)], tile.at[pl.ds(light * rows, rows)], tile_sem.at[light]
+            )
+            for light in range(lights)
+        ]
+        for read in reads:
+            read.start()
+        for read in reads:
+            read.wait()
+
+        def products(index, carry):
+            some = tile[:, pl.ds(pl.multiple_of(index * chunk, chunk), chunk)]
+            halves = jnp.dot(left[...], some, preferred_element_type=jnp.float32)
+            projected = (halves[:rank] + halves[rank:]).astype(jnp.bfloat16)
+            total[...] += lax.dot_general(
+                some, projected, (((1,), (1,)), ((), ())), preferred_element_type=jnp.float32
+            )
+            return carry
+
+        lax.fori_loop(0, width // chunk, products, 0)
+    image_ref[...] = (total[...] * scale).astype(image_ref.dtype)
+    for group in copies:
+        for copy in group:
+            copy.wait_send()
+
+
+def gather_lights(reflectance, pair, scale, collective_id):
+    rows, cams, width = reflectance.shape
+    lights = lax.axis_size("light")
+    parts = cams // lights
+    blocks = max(1, rows // 64)
+    rank = pair.shape[1] // 2
+    vmem, anywhere = pl.BlockSpec(memory_space=pltpu.VMEM), pl.BlockSpec(memory_space=pl.ANY)
+    dma = pltpu.SemaphoreType.DMA
+    return pl.pallas_call(
+        functools.partial(gather_kernel, lights, blocks, scale),
+        out_shape=(
+            jax.ShapeDtypeStruct((lights, rows, parts * width), reflectance.dtype),
+            jax.ShapeDtypeStruct((lights * rows, rank), jnp.bfloat16),
+        ),
+        in_specs=[anywhere, vmem],
+        out_specs=(anywhere, vmem),
+        scratch_shapes=[
+            pltpu.VMEM((2, rows // blocks, cams, width), reflectance.dtype),
+            pltpu.VMEM((cams, rows, width), reflectance.dtype),
+            pltpu.VMEM((lights * rows, width), reflectance.dtype),
+            pltpu.VMEM((2 * rank, lights * rows), jnp.bfloat16),
+            pltpu.VMEM((lights * rows, rank), jnp.float32),
+            dma((2,)), dma((parts,)), dma((lights,)),
+            dma((lights - 1, parts)), dma((lights - 1, parts)),
+            dma((lights - 1, blocks)), dma((lights - 1, blocks)),
+        ],
+        compiler_params=pltpu.CompilerParams(
+            collective_id=collective_id, has_side_effects=True, vmem_limit_bytes=40 * 1024 * 1024
+        ),
+    )(reflectance, pair)
 
 
 def exchange_kernel(lights, src_ref, dst_ref, bounce, local_sem, send_sem, recv_sem):
@@ -163,7 +299,7 @@
     )(part)
 
 
-def orthonormal_kernel(image_ref, basis_ref, pair_ref):
+def orthonormal_kernel(image_ref, basis_ref, pair_ref, whole):
     image = image_ref[...]
     rank = image.shape[1]
     inner = lax.dot_general(image, image, (((0,), (0,)), ((), ())), preferred_element_type=jnp.float32)
@@ -224,7 +360,9 @@
             image, piece, (((1,), (1,)), ((), ())), preferred_element_type=jnp.float32
         )
         basis = term if basis is None else basis + term
-    basis_ref[...] = basis
+    whole[...] = basis
+    own = basis_ref.shape[0]
+    basis_ref[...] = whole[pl.ds(pl.multiple_of(lax.axis_index("light") * own, own), own), :]
     high = basis.astype(jnp.bfloat16)
     pair_ref[:, :rank] = high
     pair_ref[:, rank:] = (basis - high.astype(jnp.float32)).astype(jnp.bfloat16)
@@ -232,15 +370,17 @@
 
 def orthonormal(image):
     rows, rank = image.shape
+    own = rows // lax.axis_size("light")
     vmem = pl.BlockSpec(memory_space=pltpu.VMEM)
     return pl.pallas_call(
         orthonormal_kernel,
         out_shape=(
-            jax.ShapeDtypeStruct((rows, rank), jnp.float32),
+            jax.ShapeDtypeStruct((own, rank), jnp.float32),
             jax.ShapeDtypeStruct((rows, 2 * rank), jnp.bfloat16),
         ),
         in_specs=[vmem],
         out_specs=(vmem, vmem),
+        scratch_shapes=[pltpu.VMEM((rows, rank), jnp.float32)],
     )(image)
 
 
@@ -248,25 +388,23 @@
     light_rows, camera_cols, pixels = reflectance.shape
     rank_total = start_basis.shape[1]
     light_count = lax.axis_size("light")
-    position = lax.axis_index("light")
     inverse_cols = 1.0 / (camera_cols * pixels * lax.axis_size("cam") * lax.axis_size("pix"))
     own_cols = camera_cols // light_count * pixels
-    blocks = reflectance.transpose(1, 0, 2).reshape(light_count, -1, light_rows, pixels)
-    every_light = exchange(blocks, 0).reshape(light_rows * light_count, own_cols)
-
     high = lax.reduce_precision(start_basis, 8, 7)
     pair = jnp.concatenate([high, start_basis - high], axis=1).astype(jnp.bfloat16)
+    every_light, image_part = gather_lights(reflectance, pair, inverse_cols, 0)
+    every_light = every_light.reshape(light_rows * light_count, own_cols)
     for iteration in range(ITERS):
-        halves = lax.dot_general(
-            pair, every_light, (((0,), (0,)), ((), ())), preferred_element_type=jnp.float32
-        )
-        projected = (halves[:rank_total] + halves[rank_total:]).astype(jnp.bfloat16)
-        image_part = lax.dot_general(
-            every_light, projected, (((1,), (1,)), ((), ())), preferred_element_type=jnp.float32
-        )
-        image_full = total_over_all((image_part * inverse_cols).astype(jnp.bfloat16), 1)
-        basis_now, pair = orthonormal(image_full)
-    basis_rows = lax.dynamic_slice_in_dim(basis_now, position * light_rows, light_rows, 0)
+        if iteration > 0:
+            halves = lax.dot_general(
+                pair, every_light, (((0,), (0,)), ((), ())), preferred_element_type=jnp.float32
+            )
+            projected = (halves[:rank_total] + halves[rank_total:]).astype(jnp.bfloat16)
+            image_part = lax.dot_general(
+                every_light, projected, (((1,), (1,)), ((), ())), preferred_element_type=jnp.float32
+            )
+            image_part = (image_part * inverse_cols).astype(jnp.bfloat16)
+        basis_rows, pair = orthonormal(total_over_all(image_part, 1))
     rank_rows = rank_total // light_count
     core = lax.dot_general(
         pair[:, :rank_total], every_light, (((0,), (0,)), ((), ())),

time: 307 us -> 294 us (0.958)
  matrix products: 27.1 us -> 18.1 us
  local copies, waits for them, and re-layouts: 16.3 us -> 7.36 us
  Pallas kernels: 258 us -> 262 us
    pallas_call x2 -> x3, Pallas kernels: 14.4 us -> 195 us  [the longest x1 181 us: gather_lights(): pl.pallas_call(functools.partial(gather_kernel, lights, blocks, scale), o...]
    pallas_call x2 -> x1, Pallas kernels: 197 us -> 22.1 us  [exchange(): pl.pallas_call(functools.partial(exchange_kernel, lights), out_shape=jax....]
    transpose x1 -> x0, local copies, waits for them, and re-layouts: 11.3 us -> none  [per_device(): reflectance.transpose(1, 0, 2).reshape(light_count, -1, light_rows, pixels)]
    dot_general x2 -> x1, matrix products: 11.9 us -> 5.94 us  [per_device(): lax.dot_general(pair, every_light, (((0,), (0,)), ((), ())), preferred_el...]
    unnamed x6 -> x4, local copies, waits for them, and re-layouts: 0.01 us -> 3.92 us
    dot_general x2 -> x1, matrix products: 9.47 us -> 6.42 us  [per_device(): lax.dot_general(every_light, projected, (((1,), (1,)), ((), ())), preferr...]
where the time goes in v4:
time: 294 us; the launch traced here: 291 us
  Pallas kernels  262 us (89%)
  matrix products  18.1 us (6%)
  local copies, waits for them, and re-layouts  7.36 us (3%)
    pallas_call x1, Pallas kernels, gather_lights(): pl.pallas_call(functools.partial(gather_kernel, lights, blocks, scale), o...  181 us
    pallas_call x2, Pallas kernels, total_over_all(): pl.pallas_call(functools.partial(total_kernel, lights, pixes, cams), out_...  45.1 us
    pallas_call x1, Pallas kernels, exchange(): pl.pallas_call(functools.partial(exchange_kernel, lights), out_shape=jax....  22.1 us
    pallas_call x2, Pallas kernels, orthonormal(): pl.pallas_call(orthonormal_kernel, out_shape=(jax.ShapeDtypeStruct((own,...  14.2 us
    dot_general x1, matrix products, per_device(): lax.dot_general(every_light, projected, (((1,), (1,)), ((), ())), preferr...  6.42 us
    dot_general x1, matrix products, per_device(): lax.dot_general(pair, every_light, (((0,), (0,)), ((), ())), preferred_el...  5.94 us

profile of v4, /device:TPU:0, one launch (start us, length us, event | category | flops | bytes accessed | tf_op | source)
XLA Modules:
  0.0 290.8 jit_solution(10214035916092159845)
XLA Ops:
  0.6 1.1 reduce-precision_convert_fusion
  1.8 0.1 pad_maximum_fusion.pair_ref
  1.8 180.6 %shard_map.41 = (bf16[4,256,4096]{2,1,0:T(8,128)(2,1)S(1)}, bf16[1024,128]{1,0:T(8,128)(2,1)S(1)}) custom-call(bf16[256,16,1024]{2,1,0:T(8,128)(2,1)} %source_ref.1, bf16[1024,256]{1,0:T(8,128)(2,1)S(1)} %pad_maximum_fusion.pair_ref), custom_call_target="tpu_custom_call" | custom-call | tf_op jit(solution)/shard_map/pallas_call | solution.py:132
  182.4 0.0 copy-start
  182.4 3.2 %copy-done = bf16[4,256,4096]{2,1,0:T(8,128)(2,1)} copy-done((bf16[4,256,4096]{2,1,0:T(8,128)(2,1)}, bf16[4,256,4096]{2,1,0:T(8,128)(2,1)S(1)}, u32[]{:S(2)}) %copy-start) | copy-done | bytes 8388632
  185.6 0.0 copy-start.1
  185.6 0.7 copy-done.1
  186.3 27.4 %shard_map.42.image_ref = bf16[1024,128]{1,0:T(8,128)(2,1)} custom-call(bf16[1024,128]{1,0:T(8,128)(2,1)} %copy-done.1), custom_call_target="tpu_custom_call" | custom-call | tf_op jit(solution)/shard_map/pallas_call | solution.py:283
  213.8 7.0 %shard_map.43 = (f32[256,128]{1,0:T(8,128)}, bf16[1024,256]{1,0:T(8,128)(2,1)}) custom-call(bf16[1024,128]{1,0:T(8,128)(2,1)} %shard_map.42.image_ref), custom_call_target="tpu_custom_call" | custom-call | tf_op jit(solution)/shard_map/pallas_call | solution.py:375
  220.8 5.9 %fusion.5 = f32[256,4096]{1,0:T(8,128)S(1)} fusion(bf16[1024,256]{1,0:T(8,128)(2,1)} %get-tuple-element.9, bf16[1024,4096]{1,0:T(8,128)(2,1)} %bitcast.8), kind=kOutput, calls=%fused_computation.11 | convolution fusion | flops 2147483648 | bytes 13107200 | tf_op jit(solution)/shard_map/dot_general | solution.py:399
  226.7 6.4 %fusion.1.part_ref = bf16[1024,128]{1,0:T(8,128)(2,1)} fusion(bf16[1024,4096]{1,0:T(8,128)(2,1)} %bitcast.9, f32[256,4096]{1,0:T(8,128)S(1)} %fusion.5), kind=kOutput, calls=%fused_computation.5 | convolution fusion | flops 1075052544 | bytes 12845056 | tf_op jit(solution)/shard_map/dot_general | solution.py:403
  233.2 17.6 %shard_map.44.image_ref = bf16[1024,128]{1,0:T(8,128)(2,1)} custom-call(bf16[1024,128]{1,0:T(8,128)(2,1)} %fusion.1.part_ref), custom_call_target="tpu_custom_call" | custom-call | tf_op jit(solution)/shard_map/pallas_call | solution.py:283
  250.8 7.2 %shard_map.45 = (f32[256,128]{1,0:T(8,128)}, bf16[1024,256]{1,0:T(8,128)(2,1)}) custom-call(bf16[1024,128]{1,0:T(8,128)(2,1)} %shard_map.44.image_ref), custom_call_target="tpu_custom_call" | custom-call | tf_op jit(solution)/shard_map/pallas_call | solution.py:375
  258.0 5.7 %convolution_convert_fusion = bf16[128,4096]{1,0:T(8,128)(2,1)} fusion(bf16[1024,4096]{1,0:T(8,128)(2,1)} %bitcast.10, bf16[1024,256]{1,0:T(8,128)(2,1)} %get-tuple-element.10), kind=kOutput, calls=%fused_computation | convolution fusion | flops 1074266112 | bytes 9699328 | tf_op jit(solution)/shard_map/dot_general | solution.py:409
  263.8 22.1 %shard_map.46 = bf16[4,32,4096]{2,1,0:T(8,128)(2,1)} custom-call(bf16[4,1,32,4096]{3,2,1,0:T(8,128)(2,1)} %bitcast.11), custom_call_target="tpu_custom_call" | custom-call | tf_op jit(solution)/shard_map/pallas_call | solution.py:189
  285.9 1.4 convert_bitcast_fusion
  287.3 1.4 copy.4
  288.7 2.1 reshape.21
Async XLA Ops:
  182.4 3.2 %copy-start = (bf16[4,256,4096]{2,1,0:T(8,128)(2,1)}, bf16[4,256,4096]{2,1,0:T(8,128)(2,1)S(1)}, u32[]{:S(2)}) copy-start(bf16[4,256,4096]{2,1,0:T(8,128)(2,1)S(1)} %get-tuple-element.7) | copy-start | bytes 25165828
  185.6 0.7 copy-start.1

commit v5 on v4

--- a/solution.py
+++ b/solution.py
@@ -17,7 +17,7 @@
     pl.semaphore_wait(barrier, len(devices))
 
 
-def gather_kernel(lights, blocks, scale, source_ref, pair_ref, every_ref, image_ref, arrived, turned, tile, left, total,
+def gather_kernel(lights, blocks, scale, source_ref, basis_ref, every_ref, image_ref, arrived, turned, tile, left, total,
                   load_sem, own_sem, tile_sem, send_sem, recv_sem, first_send, first_recv):
     me = lax.axis_index("light")
     rows, cams, width = source_ref.shape
@@ -87,7 +87,10 @@
     for copy in own:
         copy.start()
 
-    left[...] = pair_ref[...].T
+    basis = basis_ref[...]
+    high = basis.astype(jnp.bfloat16)
+    left[:rank] = high.T
+    left[rank:] = (basis - high.astype(jnp.float32)).astype(jnp.bfloat16).T
     total[...] = jnp.zeros_like(total)
     chunk = 256
     for part in range(parts):
@@ -121,12 +124,12 @@
             copy.wait_send()
 
 
-def gather_lights(reflectance, pair, scale, collective_id):
+def gather_lights(reflectance, basis, scale, collective_id):
     rows, cams, width = reflectance.shape
     lights = lax.axis_size("light")
     parts = cams // lights
     blocks = max(1, rows // 64)
-    rank = pair.shape[1] // 2
+    rank = basis.shape[1]
     vmem, anywhere = pl.BlockSpec(memory_space=pltpu.VMEM), pl.BlockSpec(memory_space=pl.ANY)
     dma = pltpu.SemaphoreType.DMA
     return pl.pallas_call(
@@ -150,7 +153,7 @@
         compiler_params=pltpu.CompilerParams(
             collective_id=collective_id, has_side_effects=True, vmem_limit_bytes=40 * 1024 * 1024
         ),
-    )(reflectance, pair)
+    )(reflectance, basis)
 
 
 def exchange_kernel(lights, src_ref, dst_ref, bounce, local_sem, send_sem, recv_sem):
@@ -198,7 +201,7 @@
             pltpu.SemaphoreType.DMA((lights - 1, parts)),
         ],
         compiler_params=pltpu.CompilerParams(
-            collective_id=collective_id, has_side_effects=True
+            collective_id=collective_id, has_side_effects=True, vmem_limit_bytes=8 * 1024 * 1024
         ),
     )(blocks)
 
@@ -294,7 +297,7 @@
             dma((plane - 1,)), dma((plane - 1,)),
         ],
         compiler_params=pltpu.CompilerParams(
-            collective_id=collective_id, has_side_effects=True
+            collective_id=collective_id, has_side_effects=True, vmem_limit_bytes=8 * 1024 * 1024
         ),
     )(part)
 
@@ -381,6 +384,7 @@
         in_specs=[vmem],
         out_specs=(vmem, vmem),
         scratch_shapes=[pltpu.VMEM((rows, rank), jnp.float32)],
+        compiler_params=pltpu.CompilerParams(vmem_limit_bytes=16 * 1024 * 1024),
     )(image)
 
 
@@ -390,9 +394,7 @@
     light_count = lax.axis_size("light")
     inverse_cols = 1.0 / (camera_cols * pixels * lax.axis_size("cam") * lax.axis_size("pix"))
     own_cols = camera_cols // light_count * pixels
-    high = lax.reduce_precision(start_basis, 8, 7)
-    pair = jnp.concatenate([high, start_basis - high], axis=1).astype(jnp.bfloat16)
-    every_light, image_part = gather_lights(reflectance, pair, inverse_cols, 0)
+    every_light, image_part = gather_lights(reflectance, start_basis, inverse_cols, 0)
     every_light = every_light.reshape(light_rows * light_count, own_cols)
     for iteration in range(ITERS):
         if iteration > 0:

time: 294 us -> 271 us (0.922)
  matrix products: 18.1 us -> 6.01 us
  Pallas kernels: 262 us -> 256 us
    dot_general x1, matrix products: 5.74 us -> 1.29 us  [per_device(): lax.dot_general(pair[:, :rank_total], every_light, (((0,), (0,)), ((), ()...]
    dot_general x1, matrix products: 6.42 us -> 2.34 us  [per_device(): lax.dot_general(every_light, projected, (((1,), (1,)), ((), ())), preferr...]
    dot_general x1, matrix products: 5.94 us -> 2.38 us  [per_device(): lax.dot_general(pair, every_light, (((0,), (0,)), ((), ())), preferred_el...]
    pallas_call x2, Pallas kernels: 45.1 us -> 42 us  [total_over_all(): pl.pallas_call(functools.partial(total_kernel, lights, pixes, cams), out_...]
where the time goes in v5:
time: 271 us; the launch traced here: 268 us
  Pallas kernels  256 us (94%)
  matrix products  6.01 us (2%)
  local copies, waits for them, and re-layouts  4.47 us (2%)
    pallas_call x1, Pallas kernels, gather_lights(): pl.pallas_call(functools.partial(gather_kernel, lights, blocks, scale), o...  181 us
    pallas_call x2, Pallas kernels, total_over_all(): pl.pallas_call(functools.partial(total_kernel, lights, pixes, cams), out_...  42 us
    pallas_call x1, Pallas kernels, exchange(): pl.pallas_call(functools.partial(exchange_kernel, lights), out_shape=jax....  21.9 us
    pallas_call x2, Pallas kernels, orthonormal(): pl.pallas_call(orthonormal_kernel, out_shape=(jax.ShapeDtypeStruct((own,...  12 us

profile of v5, /device:TPU:0, one launch (start us, length us, event | category | flops | bytes accessed | tf_op | source)
XLA Modules:
  0.0 267.8 jit_solution(276095898963055426)
XLA Ops:
  0.6 0.0 copy-start
  0.6 1.0 copy-done
  1.7 180.5 %shard_map.41 = (bf16[4,256,4096]{2,1,0:T(8,128)(2,1)S(1)}, bf16[1024,128]{1,0:T(8,128)(2,1)S(1)}) custom-call(bf16[256,16,1024]{2,1,0:T(8,128)(2,1)} %source_ref.1, f32[1024,128]{1,0:T(8,128)S(1)} %copy-done), custom_call_target="tpu_custom_call" | custom-call | tf_op jit(solution)/shard_map/pallas_call | solution.py:135
  182.2 25.9 %shard_map.42.image_ref = bf16[1024,128]{1,0:T(8,128)(2,1)S(1)} custom-call(bf16[1024,128]{1,0:T(8,128)(2,1)S(1)} %get-tuple-element.8.part_ref), custom_call_target="tpu_custom_call" | custom-call | tf_op jit(solution)/shard_map/pallas_call | solution.py:286
  208.1 5.9 %shard_map.43 = (f32[256,128]{1,0:T(8,128)}, bf16[1024,256]{1,0:T(8,128)(2,1)S(1)}) custom-call(bf16[1024,128]{1,0:T(8,128)(2,1)S(1)} %shard_map.42.image_ref), custom_call_target="tpu_custom_call" | custom-call | tf_op jit(solution)/shard_map/pallas_call | solution.py:378
  214.0 2.4 fusion.4
  216.4 2.3 fusion.1.part_ref
  218.7 16.1 %shard_map.44.image_ref = bf16[1024,128]{1,0:T(8,128)(2,1)S(1)} custom-call(bf16[1024,128]{1,0:T(8,128)(2,1)S(1)} %fusion.1.part_ref), custom_call_target="tpu_custom_call" | custom-call | tf_op jit(solution)/shard_map/pallas_call | solution.py:286
  234.8 6.1 %shard_map.45 = (f32[256,128]{1,0:T(8,128)}, bf16[1024,256]{1,0:T(8,128)(2,1)S(1)}) custom-call(bf16[1024,128]{1,0:T(8,128)(2,1)S(1)} %shard_map.44.image_ref), custom_call_target="tpu_custom_call" | custom-call | tf_op jit(solution)/shard_map/pallas_call | solution.py:378
  240.9 1.3 convolution_convert_fusion
  242.2 21.9 %shard_map.46 = bf16[4,32,4096]{2,1,0:T(8,128)(2,1)S(1)} custom-call(bf16[4,1,32,4096]{3,2,1,0:T(8,128)(2,1)S(1)} %bitcast.11), custom_call_target="tpu_custom_call" | custom-call | tf_op jit(solution)/shard_map/pallas_call | solution.py:192
  264.1 0.2 convert_bitcast_fusion
  264.4 1.4 copy.4
  265.7 2.1 reshape.21
Async XLA Ops:
  0.6 1.0 copy-start
